TPU v7x, 32 devices: a whole 2x2x4 slice. The times are simulated.
32 devices in a mesh: dp: 16 (over z, y, core), tensor: 2 (over x).
Axes of the slice: x: 2, y: 2, z: 4, core: 2. Of those that a mesh axis runs over, the one named last changes fastest.
Arguments:
- tokens: bfloat16 [16384, 768], P(('dp', 'tensor')), may hold values from -6 to 6
- query_weight: bfloat16 [768, 768], P('dp', 'tensor'), may hold values from -0.21875 to 0.21875
- query_bias: float32 [768], replicated, may hold values from -3 to 3
- key_weight: bfloat16 [768, 768], P('dp', 'tensor'), may hold values from -0.21875 to 0.21875
- value_weight: bfloat16 [768, 768], P('dp', 'tensor'), may hold values from -0.21875 to 0.21875
- value_bias: float32 [768], replicated, may hold values from -0.625 to 0.625
- output_weight: bfloat16 [768, 768], P('tensor', 'dp'), may hold values from -1.25 to 1.25
- output_bias: float32 [768], replicated, may hold values from -3 to 3
- first_gain: float32 [768], replicated, may hold values from 0.5 to 1.5
- first_shift: float32 [768], replicated, may hold values from -3 to 3
- inner_weight: bfloat16 [768, 3072], P('dp', 'tensor'), may hold values from -0.21875 to 0.21875
- inner_bias: float32 [3072], replicated, may hold values from -3 to 3
- outer_weight: bfloat16 [3072, 768], P('tensor', 'dp'), may hold values from -0.109375 to 0.109375
- outer_bias: float32 [768], replicated, may hold values from -3 to 3
- second_gain: float32 [768], replicated, may hold values from 0.5 to 1.5
- second_shift: float32 [768], replicated, may hold values from -3 to 3
- segments: int32 [16, 1024], P('dp'), may hold values from 0 to 7, never falling along the last dimension, each value on 1 to 768 neighbouring positions
- valid_length: int32 [16], P('dp'), may hold values from 512 to 1024
- cotangent: bfloat16 [16384, 768], P(('dp', 'tensor')), may hold values from -6 to 6
Outputs:
- layer_output: bfloat16 [16384, 768], P(('dp', 'tensor'))
- input_gradient: float32 [16384, 768], P(('dp', 'tensor'))
- query_weight_gradient: float32 [768, 768], P('dp', 'tensor')
- query_bias_gradient: float32 [768], replicated
- key_weight_gradient: float32 [768, 768], P('dp', 'tensor')
- value_weight_gradient: float32 [768, 768], P('dp', 'tensor')
- value_bias_gradient: float32 [768], replicated
- output_weight_gradient: float32 [768, 768], P('tensor', 'dp')
- output_bias_gradient: float32 [768], replicated
- first_gain_gradient: float32 [768], replicated
- first_shift_gradient: float32 [768], replicated
- inner_weight_gradient: float32 [768, 3072], P('dp', 'tensor')
- inner_bias_gradient: float32 [3072], replicated
- outer_weight_gradient: float32 [3072, 768], P('tensor', 'dp')
- outer_bias_gradient: float32 [768], replicated
- second_gain_gradient: float32 [768], replicated
- second_shift_gradient: float32 [768], replicated
Inputs may be any that keep to these rules, and one draw needn't show every extreme that they name: `segments`: segment numbers never fall along a sequence; a token attends only to tokens of its own document. tokens of a sequence at positions valid_length and beyond are padding: no query attends to them as keys except the token itself.
All inputs are finite; a program needn't handle non-finite values.
Results may differ from a plain program's by a relative error of at most 0.013.
Values may be sent and summed in bfloat16 or wider, within the bound.
No kernel may reach another device: no remote copies, remote signals or barrier semaphores. Data moves between devices by JAX's collectives and lax.ppermute only.
A program may use at most 128 MiB of HBM per device.

v0:
```python
import jax
import jax.numpy as jnp
from jax import lax
from jax.sharding import PartitionSpec as P

HEAD_DIM = 64
norm_epsilon = 1e-12
masked_score = -1e30


def normalize(matrix, gain, shift):
    center = matrix - jnp.mean(matrix, axis=-1, keepdims=True)
    spread = jnp.mean(center * center, axis=-1, keepdims=True)
    return center * lax.rsqrt(spread + norm_epsilon) * gain + shift


def exact_gelu(inner):
    return jax.nn.gelu(inner, approximate=False)


def block_scores(query_block, key_seq, segment_row, valid_count, first_row):
    block_rows = query_block.shape[0]
    length = key_seq.shape[0]
    scores = (
        jnp.einsum("qhd,khd->hqk", query_block, key_seq, preferred_element_type=jnp.float32) * 0.125
    )
    positions = jnp.arange(length, dtype=jnp.int32)
    query_pos = first_row + jnp.arange(block_rows, dtype=jnp.int32)
    query_seg = lax.dynamic_slice_in_dim(segment_row, first_row, block_rows)
    allowed = (query_seg[:, None] == segment_row[None, :]) & (
        (positions[None, :] < valid_count) | (query_pos[:, None] == positions[None, :])
    )
    return jnp.where(allowed[None], scores, masked_score)


def attend_sequence(pieces):
    query_seq, key_seq, value_seq, segment_row, valid_count = pieces
    length = query_seq.shape[0]
    block_rows = min(512, length)

    def one_block(block_index):
        first_row = block_index * block_rows
        query_block = lax.dynamic_slice_in_dim(query_seq, first_row, block_rows)
        masked = block_scores(query_block, key_seq, segment_row, valid_count, first_row)
        largest = jnp.max(masked, axis=-1, keepdims=True)
        totals = jnp.sum(jnp.exp(masked - largest), axis=-1, keepdims=True)
        log_total = largest + jnp.log(totals)
        probs_low = jnp.exp(masked - log_total).astype(jnp.bfloat16)
        context = jnp.einsum(
            "hqk,khd->qhd", probs_low, value_seq, preferred_element_type=jnp.float32
        )
        return (context.astype(jnp.bfloat16), log_total[..., 0])

    contexts, log_totals = lax.map(one_block, jnp.arange(length // block_rows, dtype=jnp.int32))
    return (contexts.reshape(query_seq.shape), log_totals)


def attend_backward(pieces):
    query_seq, key_seq, value_seq, segment_row, valid_count, grad_seq, log_totals = pieces
    length = query_seq.shape[0]
    block_rows = min(512, length)

    def one_block(running, inputs):
        key_grad, value_grad = running
        block_index, log_total = inputs
        first_row = block_index * block_rows
        query_block = lax.dynamic_slice_in_dim(query_seq, first_row, block_rows)
        grad_block = lax.dynamic_slice_in_dim(grad_seq, first_row, block_rows)
        masked = block_scores(query_block, key_seq, segment_row, valid_count, first_row)
        probs = jnp.exp(masked - log_total[..., None])
        probs_low = probs.astype(jnp.bfloat16)
        value_grad = value_grad + jnp.einsum(
            "hqk,qhd->khd", probs_low, grad_block, preferred_element_type=jnp.float32
        )
        d_probs = jnp.einsum(
            "qhd,khd->hqk", grad_block, value_seq, preferred_element_type=jnp.float32
        )
        row_inner = jnp.sum(probs * d_probs, axis=-1, keepdims=True)
        d_scores = (probs * (d_probs - row_inner)).astype(jnp.bfloat16)
        query_grad = (
            jnp.einsum("hqk,khd->qhd", d_scores, key_seq, preferred_element_type=jnp.float32)
            * 0.125
        )
        key_grad = (
            key_grad
            + jnp.einsum("hqk,qhd->khd", d_scores, query_block, preferred_element_type=jnp.float32)
            * 0.125
        )
        return ((key_grad, value_grad), query_grad.astype(jnp.bfloat16))

    empty = jnp.zeros(key_seq.shape, jnp.float32)
    block_ids = jnp.arange(length // block_rows, dtype=jnp.int32)
    (key_grad, value_grad), query_grads = lax.scan(
        one_block, (empty, empty), (block_ids, log_totals)
    )
    return (
        query_grads.reshape(query_seq.shape),
        key_grad.astype(jnp.bfloat16),
        value_grad.astype(jnp.bfloat16),
    )


def place_vector(local_part, whole, shard_index):
    width = local_part.shape[0]
    return lax.dynamic_update_slice_in_dim(
        jnp.zeros((whole,), jnp.float32), local_part, shard_index * width, 0
    )


def on_device(
    tokens,
    query_weight,
    query_bias,
    key_weight,
    value_weight,
    value_bias,
    output_weight,
    output_bias,
    first_gain,
    first_shift,
    inner_weight,
    inner_bias,
    outer_weight,
    outer_bias,
    second_gain,
    second_shift,
    segments,
    valid_length,
    cotangent,
):
    head_cols = query_weight.shape[1]
    hidden_cols = inner_weight.shape[1]
    local_heads = head_cols // HEAD_DIM
    shard_index = lax.axis_index("tensor")
    bias_query = lax.dynamic_slice_in_dim(query_bias, shard_index * head_cols, head_cols)
    bias_value = lax.dynamic_slice_in_dim(value_bias, shard_index * head_cols, head_cols)
    bias_inner = lax.dynamic_slice_in_dim(inner_bias, shard_index * hidden_cols, hidden_cols)
    full_query, full_key, full_value, full_output, full_inner, full_outer = (
        lax.all_gather(query_weight, "dp", axis=0, tiled=True),
        lax.all_gather(key_weight, "dp", axis=0, tiled=True),
        lax.all_gather(value_weight, "dp", axis=0, tiled=True),
        lax.all_gather(output_weight, "dp", axis=1, tiled=True),
        lax.all_gather(inner_weight, "dp", axis=0, tiled=True),
        lax.all_gather(outer_weight, "dp", axis=1, tiled=True),
    )
    group_rows = lax.all_gather(tokens, "tensor", axis=0, tiled=True)
    seq_count = segments.shape[0]
    seq_length = segments.shape[1]
    four_shape = (seq_count, seq_length, local_heads, HEAD_DIM)
    queries = (
        jnp.dot(group_rows, full_query, preferred_element_type=jnp.float32) + bias_query
    ).astype(jnp.bfloat16)
    keys_all = jnp.dot(group_rows, full_key, preferred_element_type=jnp.float32).astype(
        jnp.bfloat16
    )
    values_all = (
        jnp.dot(group_rows, full_value, preferred_element_type=jnp.float32) + bias_value
    ).astype(jnp.bfloat16)
    queries = queries.reshape(four_shape)
    keys_all = keys_all.reshape(four_shape)
    values_all = values_all.reshape(four_shape)
    contexts, log_totals = lax.map(
        attend_sequence, (queries, keys_all, values_all, segments, valid_length)
    )
    context = contexts.reshape(seq_count * seq_length, head_cols)
    partial_attn = jnp.dot(context, full_output, preferred_element_type=jnp.float32)
    attended = lax.psum_scatter(partial_attn, "tensor", scatter_dimension=0, tiled=True)
    first_sum = tokens.astype(jnp.float32) + attended + output_bias
    hidden = normalize(first_sum, first_gain, first_shift)
    ffn_rows = lax.all_gather(hidden.astype(jnp.bfloat16), "tensor", axis=0, tiled=True)
    inner = jnp.dot(ffn_rows, full_inner, preferred_element_type=jnp.float32) + bias_inner
    activated = exact_gelu(inner).astype(jnp.bfloat16)
    partial_ffn = jnp.dot(activated, full_outer, preferred_element_type=jnp.float32)
    outer = lax.psum_scatter(partial_ffn, "tensor", scatter_dimension=0, tiled=True)
    second_sum = hidden + outer + outer_bias
    final = normalize(second_sum, second_gain, second_shift)
    layer_output = final.astype(jnp.bfloat16)
    second_value, second_pull = jax.vjp(normalize, second_sum, second_gain, second_shift)
    d_second, second_gain_grad, second_shift_grad = second_pull(cotangent.astype(jnp.float32))
    outer_bias_grad = jnp.sum(d_second, axis=0)
    d_outer = d_second.astype(jnp.bfloat16)
    held = lax.optimization_barrier(
        (query_weight, key_weight, value_weight, output_weight, inner_weight, outer_weight, d_outer)
    )
    d_outer = held[6]
    back_query, back_key, back_value, back_output, back_inner, back_outer = (
        lax.all_gather(held[0], "dp", axis=0, tiled=True),
        lax.all_gather(held[1], "dp", axis=0, tiled=True),
        lax.all_gather(held[2], "dp", axis=0, tiled=True),
        lax.all_gather(held[3], "dp", axis=1, tiled=True),
        lax.all_gather(held[4], "dp", axis=0, tiled=True),
        lax.all_gather(held[5], "dp", axis=1, tiled=True),
    )
    outer_grad_rows = lax.all_gather(d_outer, "tensor", axis=0, tiled=True)
    outer_weight_grad = jnp.einsum(
        "gf,gd->fd", activated, outer_grad_rows, preferred_element_type=jnp.float32
    )
    d_activated = jnp.einsum(
        "gd,fd->gf", outer_grad_rows, back_outer, preferred_element_type=jnp.float32
    )
    gelu_value, gelu_pull = jax.vjp(exact_gelu, inner)
    d_inner = gelu_pull(d_activated)[0].astype(jnp.bfloat16)
    inner_weight_grad = jnp.einsum(
        "gd,gf->df", ffn_rows, d_inner, preferred_element_type=jnp.float32
    )
    inner_bias_local = jnp.sum(d_inner, axis=0, dtype=jnp.float32)
    partial_hidden = jnp.einsum(
        "gf,df->gd", d_inner, back_inner, preferred_element_type=jnp.float32
    )
    d_hidden = d_second + lax.psum_scatter(
        partial_hidden, "tensor", scatter_dimension=0, tiled=True
    )
    first_value, first_pull = jax.vjp(normalize, first_sum, first_gain, first_shift)
    d_first, first_gain_grad, first_shift_grad = first_pull(d_hidden)
    output_bias_grad = jnp.sum(d_first, axis=0)
    attn_grad_rows = lax.all_gather(d_first.astype(jnp.bfloat16), "tensor", axis=0, tiled=True)
    output_weight_grad = jnp.einsum(
        "gc,gd->cd", context, attn_grad_rows, preferred_element_type=jnp.float32
    )
    d_context = jnp.einsum(
        "gd,cd->gc", attn_grad_rows, back_output, preferred_element_type=jnp.float32
    ).astype(jnp.bfloat16)
    d_queries, d_keys, d_values = lax.map(
        attend_backward,
        (
            queries,
            keys_all,
            values_all,
            segments,
            valid_length,
            d_context.reshape(four_shape),
            log_totals,
        ),
    )
    d_queries = d_queries.reshape(seq_count * seq_length, head_cols)
    d_keys = d_keys.reshape(seq_count * seq_length, head_cols)
    d_values = d_values.reshape(seq_count * seq_length, head_cols)
    query_weight_grad = jnp.einsum(
        "gd,gc->dc", group_rows, d_queries, preferred_element_type=jnp.float32
    )
    key_weight_grad = jnp.einsum(
        "gd,gc->dc", group_rows, d_keys, preferred_element_type=jnp.float32
    )
    value_weight_grad = jnp.einsum(
        "gd,gc->dc", group_rows, d_values, preferred_element_type=jnp.float32
    )
    query_bias_local = jnp.sum(d_queries, axis=0, dtype=jnp.float32)
    value_bias_local = jnp.sum(d_values, axis=0, dtype=jnp.float32)
    partial_input = jnp.einsum(
        "gc,dc->gd", d_queries, back_query, preferred_element_type=jnp.float32
    )
    partial_input = partial_input + jnp.einsum(
        "gc,dc->gd", d_keys, back_key, preferred_element_type=jnp.float32
    )
    partial_input = partial_input + jnp.einsum(
        "gc,dc->gd", d_values, back_value, preferred_element_type=jnp.float32
    )
    input_gradient = d_first + lax.psum_scatter(
        partial_input.astype(jnp.bfloat16), "tensor", scatter_dimension=0, tiled=True
    ).astype(jnp.float32)
    query_shard, key_shard, value_shard, output_shard, inner_shard, outer_shard = (
        lax.psum_scatter(query_weight_grad, "dp", scatter_dimension=0, tiled=True),
        lax.psum_scatter(key_weight_grad, "dp", scatter_dimension=0, tiled=True),
        lax.psum_scatter(value_weight_grad, "dp", scatter_dimension=0, tiled=True),
        lax.psum_scatter(output_weight_grad, "dp", scatter_dimension=1, tiled=True),
        lax.psum_scatter(inner_weight_grad, "dp", scatter_dimension=0, tiled=True),
        lax.psum_scatter(outer_weight_grad, "dp", scatter_dimension=1, tiled=True),
    )
    model_width = query_bias.shape[0]
    hidden_width = inner_bias.shape[0]
    query_bias_full = place_vector(query_bias_local, model_width, shard_index)
    value_bias_full = place_vector(value_bias_local, model_width, shard_index)
    inner_bias_full = place_vector(inner_bias_local, hidden_width, shard_index)
    summed = lax.psum(
        (
            query_bias_full,
            value_bias_full,
            output_bias_grad,
            first_gain_grad,
            first_shift_grad,
            inner_bias_full,
            outer_bias_grad,
            second_gain_grad,
            second_shift_grad,
        ),
        ("dp", "tensor"),
    )
    return (
        layer_output,
        input_gradient,
        query_shard,
        summed[0],
        key_shard,
        value_shard,
        summed[1],
        output_shard,
        summed[2],
        summed[3],
        summed[4],
        inner_shard,
        summed[5],
        outer_shard,
        summed[6],
        summed[7],
        summed[8],
    )


def solution(mesh):
    placed = (
        P(("dp", "tensor"), None),
        P("dp", "tensor"),
        P(),
        P("dp", "tensor"),
        P("dp", "tensor"),
        P(),
        P("tensor", "dp"),
        P(),
        P(),
        P(),
        P("dp", "tensor"),
        P(),
        P("tensor", "dp"),
        P(),
        P(),
        P(),
        P("dp", None),
        P("dp"),
        P(("dp", "tensor"), None),
    )
    return jax.shard_map(
        on_device,
        mesh=mesh,
        in_specs=placed,
        out_specs=(
            P(("dp", "tensor"), None),
            P(("dp", "tensor"), None),
            P("dp", "tensor"),
            P(),
            P("dp", "tensor"),
            P("dp", "tensor"),
            P(),
            P("tensor", "dp"),
            P(),
            P(),
            P(),
            P("dp", "tensor"),
            P(),
            P("tensor", "dp"),
            P(),
            P(),
            P(),
        ),
        check_vma=False,
    )
```

profile of v0, /device:TPU:0, one launch (start us, length us, event | category | flops | bytes accessed | tf_op | source)
XLA Modules:
  0.0 1077.9 jit_solution(17472114728465103642)
XLA Ops:
  10.3 25.1 %all_gather.49 = bf16[768,384]{1,0:T(8,128)(2,1)S(1)} all-gather(bf16[48,384]{1,0:T(8,128)(2,1)} %param.24), channel_id=1, replica_groups=mesh['dp'=16,'tensor'=2] {'dp'}, dimensions={0}, use_global_device_ids=true | all-gather | bytes 626688 | tf_op jit(solution)/shard_map/all_gather | solution.py:139
  35.4 19.3 %all_gather.50 = bf16[768,384]{1,0:T(8,128)(2,1)S(1)} all-gather(bf16[48,384]{1,0:T(8,128)(2,1)} %param.26), channel_id=1, replica_groups=mesh['dp'=16,'tensor'=2] {'dp'}, dimensions={0}, use_global_device_ids=true | all-gather | bytes 626688 | tf_op jit(solution)/shard_map/all_gather | solution.py:140
  54.7 20.7 %all_gather.51 = bf16[768,384]{1,0:T(8,128)(2,1)S(1)} all-gather(bf16[48,384]{1,0:T(8,128)(2,1)} %param.27), channel_id=1, replica_groups=mesh['dp'=16,'tensor'=2] {'dp'}, dimensions={0}, use_global_device_ids=true | all-gather | bytes 626688 | tf_op jit(solution)/shard_map/all_gather | solution.py:141
  75.4 20.7 %all_gather.52 = bf16[384,768]{0,1:T(8,128)(2,1)} all-gather(bf16[384,48]{0,1:T(8,128)(2,1)} %param.29), channel_id=1, replica_groups=mesh['dp'=16,'tensor'=2] {'dp'}, dimensions={1}, use_global_device_ids=true | all-gather | bytes 626688 | tf_op jit(solution)/shard_map/all_gather | solution.py:142
  100.2 34.8 %while.47 = (s32[]{:T(128)}, bf16[2,512,6,64]{1,3,2,0:T(8,128)(2,1)S(1)}, f32[2,6,512]{2,1,0:T(8,128)S(1)}, s32[2]{0:T(128)S(1)}, s32[1024]{0:T(1024)S(1)}, /*in...) while((s32[]{:T(128)}, ...), condition=%wide.region_3.4_spmd, body=%wide.region_0.3_spmd.sunk | while | flops 842201600 | bytes 92672240 | solution.py:54
  109.8 7.8 fusion.126
  127.3 7.8 fusion.126
  140.5 41.1 %reduce-scatter.17.cloned.1.call-done = f32[512,768]{1,0:T(8,128)} async-done(((f32[1024,768]{1,0:T(8,128)}), f32[512,768]{1,0:T(8,128)}) %reduce-scatter.17.cloned.1.call-update) | async-done | bytes 1572880 | tf_op jit(solution)/shard_map/reduce_scatter | solution.py:167
  185.7 26.4 %all-gather.11.cloned.1.call-done = bf16[1024,768]{1,0:T(8,128)(2,1)} async-done(((bf16[512,768]{1,0:T(8,128)(2,1)}), bf16[1024,768]{1,0:T(8,128)(2,1)}) %all-gather.11.cloned.1.call-update) | async-done | bytes 1572880 | tf_op jit(solution)/shard_map/all_gather | solution.py:170
  212.1 19.9 %multiply_convert_fusion.1 = (bf16[1024,1536]{1,0:T(8,128)(2,1)}, f32[1024,1536]{1,0:T(8,128)}, f32[1024,1536]{1,0:T(8,128)}) fusion(f32[1536]{0:T(1024)S(1)} %dynamic_slice.65, bf16[1024,768]{1,0:T(8,128)(2,1)} %all-gather.11.cloned.1.call-done, bf16[768,1536]{1,0:T(8,128)(2,1)} %all-gather.13.cloned.1.call-done), kind=kOutput, calls=%fused_computation.55 | convolution fusion | flops 2519728128 | bytes 19666944 | tf_op jit(solution)/shard_map/dot_general | solution.py:171
  232.0 24.9 %all-gather.15.cloned.1.call-done = bf16[1536,768]{0,1:T(8,128)(2,1)} async-done(((bf16[1536,48]{0,1:T(8,128)(2,1)}), bf16[1536,768]{0,1:T(8,128)(2,1)}) %all-gather.15.cloned.1.call-update) | async-done | bytes 2359312 | tf_op jit(solution)/shard_map/all_gather | solution.py:144
  256.9 6.9 fusion.55
  263.9 41.9 %reduce-scatter.19.cloned.1.call-done = f32[512,768]{1,0:T(8,128)} async-done(((f32[1024,768]{1,0:T(8,128)}), f32[512,768]{1,0:T(8,128)}) %reduce-scatter.19.cloned.1.call-update) | async-done | bytes 1572880 | tf_op jit(solution)/shard_map/reduce_scatter | solution.py:174
  315.8 25.2 %all-gather.17.cloned.1.call-done = bf16[1024,768]{1,0:T(8,128)(2,1)} async-done(((bf16[512,768]{1,0:T(8,128)(2,1)}), bf16[1024,768]{1,0:T(8,128)(2,1)}) %all-gather.17.cloned.1.call-update) | async-done | bytes 1572880 | tf_op jit(solution)/shard_map/all_gather | solution.py:194
  341.0 45.0 %all-gather.19.cloned.1.call-done = bf16[1536,768]{0,1:T(8,128)(2,1)} async-done(((bf16[1536,48]{0,1:T(8,128)(2,1)}), bf16[1536,768]{0,1:T(8,128)(2,1)}) %all-gather.19.cloned.1.call-update) | async-done | bytes 2359312 | tf_op jit(solution)/shard_map/all_gather | solution.py:192
  385.9 12.4 %convert_reduce_fusion = (f32[1536]{0:T(1024)}, bf16[1024,1536]{1,0:T(8,128)(2,1)}) fusion(f32[1024,1536]{1,0:T(8,128)} %get-tuple-element.366, f32[1024,1536]{1,0:T(8,128)} %get-tuple-element.378, f32[1536]{0:T(1024)S(1)} %dynamic_slice.65, bf16[1024,768]{1,0:T(8,128)(2,1)} %all-gather.17.cloned.1.call-done, ...), kind=kOutput, calls=%fused_computation.53 | convolution fusion | flops 2442656256 | bytes 19673088 | tf_op jit(solution)/shard_map/gd,fd->gf/dot_general | solution.py:198
  398.4 30.9 %all-gather.21.cloned.1.call-done = bf16[768,1536]{1,0:T(8,128)(2,1)} async-done(((bf16[48,1536]{1,0:T(8,128)(2,1)}), bf16[768,1536]{1,0:T(8,128)(2,1)}) %all-gather.21.cloned.1.call-update) | async-done | bytes 2359312 | tf_op jit(solution)/shard_map/all_gather | solution.py:191
  436.2 41.9 %reduce-scatter.21.cloned.1.call-done = f32[512,768]{1,0:T(8,128)} async-done(((f32[1024,768]{1,0:T(8,128)}), f32[512,768]{1,0:T(8,128)}) %reduce-scatter.21.cloned.1.call-update) | async-done | bytes 1572880 | tf_op jit(solution)/shard_map/reduce_scatter | solution.py:210
  485.0 23.1 %all_gather.60 = bf16[384,768]{0,1:T(8,128)(2,1)S(1)} all-gather(bf16[384,48]{0,1:T(8,128)(2,1)S(1)} %copy-done.23), channel_id=1, replica_groups=mesh['dp'=16,'tensor'=2] {'dp'}, dimensions={1}, use_global_device_ids=true | all-gather | bytes 626688 | tf_op jit(solution)/shard_map/all_gather | solution.py:190
  508.1 20.4 %all_gather.61 = bf16[768,384]{1,0:T(8,128)(2,1)} all-gather(bf16[48,384]{1,0:T(8,128)(2,1)S(1)} %copy-done.24), channel_id=1, replica_groups=mesh['dp'=16,'tensor'=2] {'dp'}, dimensions={0}, use_global_device_ids=true | all-gather | bytes 626688 | tf_op jit(solution)/shard_map/all_gather | solution.py:187
  528.6 22.0 %all_gather.62 = bf16[768,384]{1,0:T(8,128)(2,1)} all-gather(bf16[48,384]{1,0:T(8,128)(2,1)S(1)} %copy-done.25), channel_id=1, replica_groups=mesh['dp'=16,'tensor'=2] {'dp'}, dimensions={0}, use_global_device_ids=true | all-gather | bytes 626688 | tf_op jit(solution)/shard_map/all_gather | solution.py:188
  550.5 20.4 %all_gather.63 = bf16[768,384]{1,0:T(8,128)(2,1)} all-gather(bf16[48,384]{1,0:T(8,128)(2,1)S(1)} %copy-done.26), channel_id=1, replica_groups=mesh['dp'=16,'tensor'=2] {'dp'}, dimensions={0}, use_global_device_ids=true | all-gather | bytes 626688 | tf_op jit(solution)/shard_map/all_gather | solution.py:189
  575.1 57.7 %while.48 = (s32[]{:T(128)}, f32[1024,6,64]{0,2,1:T(8,128)S(1)}, f32[1024,6,64]{0,2,1:T(8,128)}, bf16[2,512,6,64]{1,3,2,0:T(8,128)(2,1)}, s32[2]{0:T(128)S(1)}, ...) while((s32[]{:T(128)}, f32[1024,6,64]{0,2,1:T(8,128)S(1)}, ...), condition=%wide.region_17.18_spmd.clone, body=%wide.region_15.17_spmd.clone.sunk | while | flops 2064906752 | bytes 144941456 | solution.py:93
  641.3 7.1 fusion.61
  648.5 7.2 fusion.60
  673.5 39.8 %all-reduce = (f32[768]{0:T(1024)}, f32[768]{0:T(1024)}, f32[768]{0:T(1024)}, f32[768]{0:T(1024)}, f32[768]{0:T(1024)}, /*index=5*/f32[3072]{0:T(1024)}, f32[768]{0:T(1024)}, f32[768]{0:T(1024)}, f32[768]{0:T(1024)}) all-reduce(f32[768]{0:T(1024)S(1)} %dynamic_update_slice.32, ...), channel_id=1, replica_groups=mesh['dp'=16,'tensor'=2] {'dp','tensor'}, use_global_device_ids=true, to_apply=%region_21.22 | all-reduce | flops 9216 | bytes 73728 | tf_op jit(solution)/shard_map/psum | solution.py:274
  715.8 29.6 %reduce-scatter.29.cloned.1.call-done = f32[1536,48]{0,1:T(8,128)} async-done(((f32[1536,768]{0,1:T(8,128)}), f32[1536,48]{0,1:T(8,128)}) %reduce-scatter.29.cloned.1.call-update) | async-done | bytes 294928 | tf_op jit(solution)/shard_map/reduce_scatter | solution.py:267
  745.5 79.0 %reduce-scatter.27.cloned.1.call-done = f32[48,1536]{1,0:T(8,128)} async-done(((f32[768,1536]{1,0:T(8,128)}), f32[48,1536]{1,0:T(8,128)}) %reduce-scatter.27.cloned.1.call-update) | async-done | bytes 294928 | tf_op jit(solution)/shard_map/reduce_scatter | solution.py:266
  824.4 61.6 %reduce-scatter.25.cloned.1.call-done = f32[384,48]{0,1:T(8,128)} async-done(((f32[384,768]{0,1:T(8,128)}), f32[384,48]{0,1:T(8,128)}) %reduce-scatter.25.cloned.1.call-update) | async-done | bytes 73744 | tf_op jit(solution)/shard_map/reduce_scatter | solution.py:265
  886.1 61.4 %reduce-scatter.35.cloned.1.call-done = f32[48,384]{1,0:T(8,128)} async-done(((f32[768,384]{1,0:T(8,128)}), f32[48,384]{1,0:T(8,128)}) %reduce-scatter.35.cloned.1.call-update) | async-done | bytes 73744
  947.4 61.5 %reduce-scatter.31.cloned.1.call-done = f32[48,384]{1,0:T(8,128)} async-done(((f32[768,384]{1,0:T(8,128)}), f32[48,384]{1,0:T(8,128)}) %reduce-scatter.31.cloned.1.call-update) | async-done | bytes 73744
  1008.9 61.2 %reduce-scatter.33.cloned.1.call-done = f32[48,384]{1,0:T(8,128)} async-done(((f32[768,384]{1,0:T(8,128)}), f32[48,384]{1,0:T(8,128)}) %reduce-scatter.33.cloned.1.call-update) | async-done | bytes 73744
  (231 shorter events, 145.7 us)
Async XLA Ops:
  8.0 88.0 %all-gather.9.cloned.1.call-start = ((), (), s32[]{:S(2)}) async-start(), calls=%async_computation.10 | async-start | bytes 2359296 | tf_op jit(solution)/shard_map/all_gather | solution.py:146
  8.8 172.9 %reduce-scatter.17.cloned.1.call-start = ((), (), s32[]{:S(2)}) async-start(), calls=%async_computation.11 | async-start | bytes 4718592 | tf_op jit(solution)/shard_map/reduce_scatter | solution.py:167
  137.0 44.7 %copy-start.13 = (bf16[512,768]{1,0:T(8,128)(2,1)S(1)}, bf16[512,768]{1,0:T(8,128)(2,1)}, u32[]{:S(2)}) copy-start(bf16[512,768]{1,0:T(8,128)(2,1)} %param.23) | copy-start | bytes 2359300
  137.0 44.7 %copy-start.36 = (f32[768]{0:T(1024)S(1)}, f32[768]{0:T(1024)}, u32[]{:S(2)}) copy-start(f32[768]{0:T(1024)} %param.30) | copy-start | bytes 9220
  139.7 44.1 %copy-start.27 = (f32[768]{0:T(1024)S(1)}, f32[768]{0:T(1024)}, u32[]{:S(2)}) copy-start(f32[768]{0:T(1024)} %param.31) | copy-start | bytes 9220
  139.7 44.1 %copy-start.33 = (f32[768]{0:T(1024)S(1)}, f32[768]{0:T(1024)}, u32[]{:S(2)}) copy-start(f32[768]{0:T(1024)} %param.32) | copy-start | bytes 9220
  139.7 46.0 %all-gather.13.cloned.1.call-start = ((), (), s32[]{:S(2)}) async-start(), calls=%async_computation.13 | async-start | bytes 2506752 | tf_op jit(solution)/shard_map/all_gather | solution.py:143
  140.3 71.8 %all-gather.11.cloned.1.call-start = ((), (), s32[]{:S(2)}) async-start(), calls=%async_computation.12 | async-start | bytes 2359296 | tf_op jit(solution)/shard_map/all_gather | solution.py:170
  185.0 72.0 %all-gather.15.cloned.1.call-start = ((), (), s32[]{:S(2)}) async-start(), calls=%async_computation.14 | async-start | bytes 2506752 | tf_op jit(solution)/shard_map/all_gather | solution.py:144
  185.5 120.2 %reduce-scatter.19.cloned.1.call-start = ((), (), s32[]{:S(2)}) async-start(), calls=%async_computation.15 | async-start | bytes 4718592 | tf_op jit(solution)/shard_map/reduce_scatter | solution.py:174
  263.8 42.0 %copy-start.37 = (f32[768]{0:T(1024)S(1)}, f32[768]{0:T(1024)}, u32[]{:S(2)}) copy-start(f32[768]{0:T(1024)} %param.36) | copy-start | bytes 9220
  263.8 44.3 %copy-start.12 = (bf16[512,768]{1,0:T(8,128)(2,1)S(1)}, bf16[512,768]{1,0:T(8,128)(2,1)}, u32[]{:S(2)}) copy-start(bf16[512,768]{1,0:T(8,128)(2,1)} %param.41) | copy-start | bytes 2359300
  263.9 44.3 %copy-start.30 = (f32[768]{0:T(1024)S(1)}, f32[768]{0:T(1024)}, u32[]{:S(2)}) copy-start(f32[768]{0:T(1024)} %param.37) | copy-start | bytes 9220
  263.9 77.1 %all-gather.17.cloned.1.call-start = ((), (), s32[]{:S(2)}) async-start(), calls=%async_computation.16 | async-start | bytes 2359296 | tf_op jit(solution)/shard_map/all_gather | solution.py:194
  313.8 72.1 %all-gather.19.cloned.1.call-start = ((), (), s32[]{:S(2)}) async-start(), calls=%async_computation.17 | async-start | bytes 2506752 | tf_op jit(solution)/shard_map/all_gather | solution.py:192
  314.6 114.7 %all-gather.21.cloned.1.call-start = ((), (), s32[]{:S(2)}) async-start(), calls=%async_computation.18 | async-start | bytes 2506752 | tf_op jit(solution)/shard_map/all_gather | solution.py:191
  315.3 162.8 %reduce-scatter.21.cloned.1.call-start = ((), (), s32[]{:S(2)}) async-start(), calls=%async_computation.19 | async-start | bytes 4718592 | tf_op jit(solution)/shard_map/reduce_scatter | solution.py:210
  436.2 134.8 %all-gather.23.cloned.1.call-start = ((), (), s32[]{:S(2)}) async-start(), calls=%async_computation.20 | async-start | bytes 2359296 | tf_op jit(solution)/shard_map/all_gather | solution.py:216
  482.1 26.0 %copy-start.24 = (bf16[48,384]{1,0:T(8,128)(2,1)S(1)}, bf16[48,384]{1,0:T(8,128)(2,1)}, u32[]{:S(2)}) copy-start(bf16[48,384]{1,0:T(8,128)(2,1)} %param.24) | copy-start | bytes 110596
  482.1 46.5 %copy-start.25 = (bf16[48,384]{1,0:T(8,128)(2,1)S(1)}, bf16[48,384]{1,0:T(8,128)(2,1)}, u32[]{:S(2)}) copy-start(bf16[48,384]{1,0:T(8,128)(2,1)} %param.26) | copy-start | bytes 110596
  482.1 68.4 %copy-start.26 = (bf16[48,384]{1,0:T(8,128)(2,1)S(1)}, bf16[48,384]{1,0:T(8,128)(2,1)}, u32[]{:S(2)}) copy-start(bf16[48,384]{1,0:T(8,128)(2,1)} %param.27) | copy-start | bytes 110596
  484.9 228.4 %reduce-scatter.23.cloned.1.call-start = ((), (), s32[]{:S(2)}) async-start(), calls=%async_computation.21 | async-start | bytes 2359296 | tf_op jit(solution)/shard_map/reduce_scatter | solution.py:258
  596.0 5.9 copy-start.1
  596.0 5.9 copy-start.5
  641.2 104.2 %reduce-scatter.29.cloned.1.call-start = ((), (), s32[]{:S(2)}) async-start(), calls=%async_computation.24 | async-start | bytes 5013504 | tf_op jit(solution)/shard_map/reduce_scatter | solution.py:267
  648.4 176.0 %reduce-scatter.27.cloned.1.call-start = ((), (), s32[]{:S(2)}) async-start(), calls=%async_computation.23 | async-start | bytes 5013504 | tf_op jit(solution)/shard_map/reduce_scatter | solution.py:266
  655.7 230.4 %reduce-scatter.25.cloned.1.call-start = ((), (), s32[]{:S(2)}) async-start(), calls=%async_computation.22 | async-start | bytes 1253376 | tf_op jit(solution)/shard_map/reduce_scatter | solution.py:265
  660.4 287.1 %reduce-scatter.35.cloned.1.call-start = ((), (), s32[]{:S(2)}) async-start(), calls=%async_computation.27 | async-start | bytes 1253376
  664.1 344.8 %reduce-scatter.31.cloned.1.call-start = ((), (), s32[]{:S(2)}) async-start(), calls=%async_computation.25 | async-start | bytes 1253376
  667.8 402.3 %reduce-scatter.33.cloned.1.call-start = ((), (), s32[]{:S(2)}) async-start(), calls=%async_computation.26 | async-start | bytes 1253376
  670.4 43.0 %copy-start.8 = (f32[512,768]{1,0:T(8,128)S(1)}, f32[512,768]{1,0:T(8,128)}, u32[]{:S(2)}) copy-start(f32[512,768]{1,0:T(8,128)} %copy-done.7) | copy-start | bytes 4718596
  670.4 42.9 %copy-start.29 = (f32[512]{0:T(512)S(1)}, f32[512]{0:T(512)}, u32[]{:S(2)}) copy-start(f32[512]{0:T(512)} %copy-done.28) | copy-start | bytes 6148
  (31 other events, 98.1 us)
Sparse Core Ops, SparseCore 0:
  10.4 29.8 all-gather.8
  139.8 41.8 reduce-scatter.16
  264.0 41.7 reduce-scatter.18
  436.3 41.7 reduce-scatter.20
  485.0 27.1 all-gather.22
Sparse Core Ops, SparseCore 1:
  142.5 40.8 all-gather.12
  185.3 26.7 all-gather.10
  214.3 42.6 all-gather.14
  313.9 27.0 all-gather.16
  343.3 42.6 all-gather.18
  388.2 40.9 all-gather.20
  641.3 23.6 reduce-scatter.22
  669.3 76.1 reduce-scatter.28
  749.8 74.6 reduce-scatter.26
  828.7 57.3 reduce-scatter.24
  890.1 57.2 reduce-scatter.34
  951.6 57.2 reduce-scatter.30
  1013.0 57.1 reduce-scatter.32
where the time goes:
time: 1090 us; the launch traced here: 1080 us
  waiting for transfers between devices  635 us (58%)
  blocking collectives  212 us (19%)
  matrix products  147 us (13%)
  other arithmetic  42.9 us (4%)
  local copies, waits for them, and re-layouts  20.5 us (2%)
  between operations  16.7 us (2%)
    unnamed x21, waiting for transfers between devices  187 us
    reduce_scatter x1, waiting for transfers between devices, on_device(): lax.psum_scatter(inner_weight_grad, 'dp', scatter_dimension=0, tiled=True)  79 us
    reduce_scatter x1, waiting for transfers between devices, on_device(): lax.psum_scatter(output_weight_grad, 'dp', scatter_dimension=1, tiled=True)  61.6 us
    all_gather x1, waiting for transfers between devices, on_device(): lax.all_gather(held[5], 'dp', axis=1, tiled=True)  45 us
    reduce_scatter x1, waiting for transfers between devices, on_device(): lax.psum_scatter(partial_hidden, 'tensor', scatter_dimension=0, tiled=True)  41.9 us
    reduce_scatter x1, waiting for transfers between devices, on_device(): lax.psum_scatter(partial_ffn, 'tensor', scatter_dimension=0, tiled=True)  41.9 us
    reduce_scatter x1, waiting for transfers between devices, on_device(): lax.psum_scatter(partial_attn, 'tensor', scatter_dimension=0, tiled=True)  41.1 us
    psum x1, blocking collectives, on_device(): lax.psum((query_bias_full, value_bias_full, output_bias_grad, first_gain_...  39.8 us
  transfers between devices with their start and end apart: 18, of which 14 were waited for; matrix products, arithmetic and copies ran while one was open for 6% of the time, Pallas kernels for 0%

commit v1 on v0

--- a/solution.py
+++ b/solution.py
@@ -6,6 +6,12 @@
 HEAD_DIM = 64
 norm_epsilon = 1e-12
 masked_score = -1e30
+
+
+def work_pages(t0, axis_k):
+    t0 = jnp.moveaxis(t0, 0, axis_k)
+    s_next = t0.shape
+    return t0.reshape(*s_next[:axis_k], s_next[axis_k] * s_next[axis_k + 1], *s_next[axis_k + 2 :])
 
 
 def normalize(matrix, gain, shift):
@@ -183,13 +189,35 @@
         (query_weight, key_weight, value_weight, output_weight, inner_weight, outer_weight, d_outer)
     )
     d_outer = held[6]
+
+    def derive_ranges(panel, device_axis, join_dim=1):
+        n_blocks = lax.psum(1, axis_name=device_axis)
+        crops = tuple(((h, (h + 1) % n_blocks) for h in range(n_blocks)))
+        series = tuple(((s, rr) for rr, s in crops))
+        front, f_now = ([], [])
+        for dev in [*range(n_blocks - 1)]:
+            if dev % 2 == 0:
+                r2 = lax.ppermute(front[-1] if front else panel, device_axis, perm=crops)
+                front.append(r2)
+            else:
+                local_out = lax.ppermute(
+                    f_now[-1] if f_now else panel, axis_name=device_axis, perm=series
+                )
+                f_now.append(local_out)
+        last = jnp.stack([*front[::-1], panel, *f_now], axis=0)
+        w2 = lax.axis_index(device_axis)
+        latest = len(front)
+        parts_out = w2 - latest
+        last = last[(jnp.arange(n_blocks) - parts_out) % n_blocks]
+        return work_pages(last, join_dim)
+
     back_query, back_key, back_value, back_output, back_inner, back_outer = (
         lax.all_gather(held[0], "dp", axis=0, tiled=True),
         lax.all_gather(held[1], "dp", axis=0, tiled=True),
         lax.all_gather(held[2], "dp", axis=0, tiled=True),
         lax.all_gather(held[3], "dp", axis=1, tiled=True),
         lax.all_gather(held[4], "dp", axis=0, tiled=True),
-        lax.all_gather(held[5], "dp", axis=1, tiled=True),
+        derive_ranges(held[5], "dp"),
     )
     outer_grad_rows = lax.all_gather(d_outer, "tensor", axis=0, tiled=True)
     outer_weight_grad = jnp.einsum(

time: 1090 us -> 1070 us (0.982)
  waiting for transfers between devices: 635 us -> 565 us
  starting transfers between devices: 1.63 us -> 33.2 us
  local copies, waits for them, and re-layouts: 20.5 us -> 42.5 us
    all_gather x1 -> x0, waiting for transfers between devices: 45 us -> none  [on_device(): lax.all_gather(held[5], 'dp', axis=1, tiled=True)]
    ppermute x0 -> x15, starting transfers between devices: none -> 32 us  [the longest x7 31.9 us: derive_ranges(): lax.ppermute(f_now[-1] if f_now else panel, axis_name=device_axis, perm=s...]
    all_gather x1, waiting for transfers between devices: 30.9 us -> 1.09 us  [on_device(): lax.all_gather(held[4], 'dp', axis=0, tiled=True)]
    ppermute x0 -> x15, waiting for transfers between devices: none -> 27.3 us  [the longest x8 27.2 us: derive_ranges(): r2 = lax.ppermute(front[-1] if front else panel, device_axis, perm=crops)]
    all_gather x1, waiting for transfers between devices: 25.2 us -> 0.01 us  [on_device(): outer_grad_rows = lax.all_gather(d_outer, 'tensor', axis=0, tiled=True)]
    unnamed x71 -> x100, local copies, waits for them, and re-layouts: 8.76 us -> 27.8 us
    unnamed x21 -> x20, waiting for transfers between devices: 187 us -> 186 us
  transfers between devices with their start and end apart: 18 -> 32, of which waited for: 14 -> 21; matrix products, arithmetic and copies ran while one was open for 6% -> 8% of each run, Pallas kernels for 0% -> 0%
where the time goes in v1:
time: 1070 us; the launch traced here: 1060 us
  waiting for transfers between devices  565 us (53%)
  blocking collectives  211 us (20%)
  matrix products  144 us (13%)
  other arithmetic  42.9 us (4%)
  local copies, waits for them, and re-layouts  42.5 us (4%)
  starting transfers between devices  33.2 us (3%)
  between operations  16.7 us (2%)
    unnamed x20, waiting for transfers between devices  186 us
    reduce_scatter x1, waiting for transfers between devices, on_device(): lax.psum_scatter(inner_weight_grad, 'dp', scatter_dimension=0, tiled=True)  79 us
    reduce_scatter x1, waiting for transfers between devices, on_device(): lax.psum_scatter(output_weight_grad, 'dp', scatter_dimension=1, tiled=True)  61.9 us
    reduce_scatter x1, waiting for transfers between devices, on_device(): lax.psum_scatter(partial_hidden, 'tensor', scatter_dimension=0, tiled=True)  41.9 us
    reduce_scatter x1, waiting for transfers between devices, on_device(): lax.psum_scatter(partial_ffn, 'tensor', scatter_dimension=0, tiled=True)  41.9 us
    reduce_scatter x1, waiting for transfers between devices, on_device(): lax.psum_scatter(partial_attn, 'tensor', scatter_dimension=0, tiled=True)  41.2 us
    psum x1, blocking collectives, on_device(): lax.psum((query_bias_full, value_bias_full, output_bias_grad, first_gain_...  39.2 us
    reduce_scatter x1, waiting for transfers between devices, on_device(): lax.psum_scatter(outer_weight_grad, 'dp', scatter_dimension=1, tiled=True)  32.7 us
  transfers between devices with their start and end apart: 32, of which 21 were waited for; matrix products, arithmetic and copies ran while one was open for 8% of the time, Pallas kernels for 0%

profile of v1, /device:TPU:0, one launch (start us, length us, event | category | flops | bytes accessed | tf_op | source)
XLA Modules:
  0.0 1057.5 jit_solution(14836828708076920084)
XLA Ops:
  10.4 25.1 %all_gather.46 = bf16[768,384]{1,0:T(8,128)(2,1)S(1)} all-gather(bf16[48,384]{1,0:T(8,128)(2,1)} %param.24), channel_id=1, replica_groups=mesh['dp'=16,'tensor'=2] {'dp'}, dimensions={0}, use_global_device_ids=true | all-gather | bytes 626688 | tf_op jit(solution)/shard_map/all_gather | solution.py:145
  35.4 19.3 %all_gather.47 = bf16[768,384]{1,0:T(8,128)(2,1)S(1)} all-gather(bf16[48,384]{1,0:T(8,128)(2,1)} %param.26), channel_id=1, replica_groups=mesh['dp'=16,'tensor'=2] {'dp'}, dimensions={0}, use_global_device_ids=true | all-gather | bytes 626688 | tf_op jit(solution)/shard_map/all_gather | solution.py:146
  54.7 20.7 %all_gather.48 = bf16[768,384]{1,0:T(8,128)(2,1)S(1)} all-gather(bf16[48,384]{1,0:T(8,128)(2,1)} %param.27), channel_id=1, replica_groups=mesh['dp'=16,'tensor'=2] {'dp'}, dimensions={0}, use_global_device_ids=true | all-gather | bytes 626688 | tf_op jit(solution)/shard_map/all_gather | solution.py:147
  75.4 20.4 %all_gather.49 = bf16[384,768]{0,1:T(8,128)(2,1)} all-gather(bf16[384,48]{0,1:T(8,128)(2,1)S(1)} %copy-done.25), channel_id=1, replica_groups=mesh['dp'=16,'tensor'=2] {'dp'}, dimensions={1}, use_global_device_ids=true | all-gather | bytes 626688 | tf_op jit(solution)/shard_map/all_gather | solution.py:148
  100.0 34.8 %while.47 = (s32[]{:T(128)}, bf16[2,512,6,64]{1,3,2,0:T(8,128)(2,1)S(1)}, f32[2,6,512]{2,1,0:T(8,128)S(1)}, s32[2]{0:T(128)S(1)}, s32[1024]{0:T(1024)S(1)}, /*in...) while((s32[]{:T(128)}, ...), condition=%wide.region_3.4_spmd, body=%wide.region_0.3_spmd.sunk | while | flops 842201600 | bytes 92672240 | solution.py:60
  109.6 7.8 fusion.128
  127.0 7.8 fusion.128
  140.2 41.2 %reduce-scatter.17.cloned.1.call-done = f32[512,768]{1,0:T(8,128)} async-done(((f32[1024,768]{1,0:T(8,128)}), f32[512,768]{1,0:T(8,128)}) %reduce-scatter.17.cloned.1.call-update) | async-done | bytes 1572880 | tf_op jit(solution)/shard_map/reduce_scatter | solution.py:173
  185.4 26.4 %all-gather.10.cloned.1.call-done = bf16[1024,768]{1,0:T(8,128)(2,1)} async-done(((bf16[512,768]{1,0:T(8,128)(2,1)}), bf16[1024,768]{1,0:T(8,128)(2,1)}) %all-gather.10.cloned.1.call-update) | async-done | bytes 1572880 | tf_op jit(solution)/shard_map/all_gather | solution.py:176
  211.9 19.9 %multiply_convert_fusion.1 = (bf16[1024,1536]{1,0:T(8,128)(2,1)}, f32[1024,1536]{1,0:T(8,128)}, f32[1024,1536]{1,0:T(8,128)}) fusion(f32[1536]{0:T(1024)S(1)} %dynamic_slice.65, bf16[1024,768]{1,0:T(8,128)(2,1)} %all-gather.10.cloned.1.call-done, bf16[768,1536]{1,0:T(8,128)(2,1)} %all-gather.12.cloned.1.call-done), kind=kOutput, calls=%fused_computation.56 | convolution fusion | flops 2519728128 | bytes 19666944 | tf_op jit(solution)/shard_map/dot_general | solution.py:177
  231.8 24.9 %all-gather.14.cloned.1.call-done = bf16[1536,768]{0,1:T(8,128)(2,1)} async-done(((bf16[1536,48]{0,1:T(8,128)(2,1)}), bf16[1536,768]{0,1:T(8,128)(2,1)}) %all-gather.14.cloned.1.call-update) | async-done | bytes 2359312 | tf_op jit(solution)/shard_map/all_gather | solution.py:150
  256.7 6.9 fusion.57
  263.7 41.9 %reduce-scatter.19.cloned.1.call-done = f32[512,768]{1,0:T(8,128)} async-done(((f32[1024,768]{1,0:T(8,128)}), f32[512,768]{1,0:T(8,128)}) %reduce-scatter.19.cloned.1.call-update) | async-done | bytes 1572880 | tf_op jit(solution)/shard_map/reduce_scatter | solution.py:180
  313.7 7.3 collective-permute-done
  394.8 12.5 %convert_reduce_fusion = (f32[1536]{0:T(1024)}, bf16[1024,1536]{1,0:T(8,128)(2,1)}) fusion(f32[1024,1536]{1,0:T(8,128)} %get-tuple-element.366, f32[1024,1536]{1,0:T(8,128)} %get-tuple-element.378, f32[1536]{0:T(1024)S(1)} %dynamic_slice.65, bf16[1024,768]{1,0:T(8,128)(2,1)} %all-gather.16.cloned.1.call-done, bf16[1536,768]{0,1:T(8,128)(2,1)} %bitcast.162), kind=kOutput, calls=%fused_computation.54 | convolution fusion | flops 2442656256 | bytes 19673088 | tf_op jit(solution)/shard_map/gd,fd->gf/dot_general | solution.py:226
  408.4 6.9 fusion.58
  415.4 41.9 %reduce-scatter.21.cloned.1.call-done = f32[512,768]{1,0:T(8,128)} async-done(((f32[1024,768]{1,0:T(8,128)}), f32[512,768]{1,0:T(8,128)}) %reduce-scatter.21.cloned.1.call-update) | async-done | bytes 1572880 | tf_op jit(solution)/shard_map/reduce_scatter | solution.py:238
  464.2 23.1 %all_gather.56 = bf16[384,768]{0,1:T(8,128)(2,1)S(1)} all-gather(bf16[384,48]{0,1:T(8,128)(2,1)S(1)} %copy-done.26), channel_id=1, replica_groups=mesh['dp'=16,'tensor'=2] {'dp'}, dimensions={1}, use_global_device_ids=true | all-gather | bytes 626688 | tf_op jit(solution)/shard_map/all_gather | solution.py:218
  487.3 20.4 %all_gather.57 = bf16[768,384]{1,0:T(8,128)(2,1)} all-gather(bf16[48,384]{1,0:T(8,128)(2,1)S(1)} %copy-done.27), channel_id=1, replica_groups=mesh['dp'=16,'tensor'=2] {'dp'}, dimensions={0}, use_global_device_ids=true | all-gather | bytes 626688 | tf_op jit(solution)/shard_map/all_gather | solution.py:215
  507.7 22.0 %all_gather.58 = bf16[768,384]{1,0:T(8,128)(2,1)} all-gather(bf16[48,384]{1,0:T(8,128)(2,1)S(1)} %copy-done.28), channel_id=1, replica_groups=mesh['dp'=16,'tensor'=2] {'dp'}, dimensions={0}, use_global_device_ids=true | all-gather | bytes 626688 | tf_op jit(solution)/shard_map/all_gather | solution.py:216
  529.7 20.4 %all_gather.59 = bf16[768,384]{1,0:T(8,128)(2,1)} all-gather(bf16[48,384]{1,0:T(8,128)(2,1)S(1)} %copy-done.29), channel_id=1, replica_groups=mesh['dp'=16,'tensor'=2] {'dp'}, dimensions={0}, use_global_device_ids=true | all-gather | bytes 626688 | tf_op jit(solution)/shard_map/all_gather | solution.py:217
  554.2 57.7 %while.48 = (s32[]{:T(128)}, f32[1024,6,64]{0,2,1:T(8,128)S(1)}, f32[1024,6,64]{0,2,1:T(8,128)}, bf16[2,512,6,64]{1,3,2,0:T(8,128)(2,1)}, s32[2]{0:T(128)S(1)}, ...) while((s32[]{:T(128)}, f32[1024,6,64]{0,2,1:T(8,128)S(1)}, ...), condition=%wide.region_17.18_spmd.clone, body=%wide.region_15.17_spmd.clone.sunk | while | flops 2064906752 | bytes 144941456 | solution.py:99
  604.4 5.9 fusion.140
  620.3 7.2 fusion.63
  627.5 7.2 fusion.62
  650.0 39.2 %all-reduce = (f32[768]{0:T(1024)}, f32[768]{0:T(1024)}, f32[768]{0:T(1024)}, f32[768]{0:T(1024)}, f32[768]{0:T(1024)}, /*index=5*/f32[3072]{0:T(1024)}, f32[768]{0:T(1024)}, f32[768]{0:T(1024)}, f32[768]{0:T(1024)}) all-reduce(f32[768]{0:T(1024)S(1)} %dynamic_update_slice.32, ...), channel_id=1, replica_groups=mesh['dp'=16,'tensor'=2] {'dp','tensor'}, use_global_device_ids=true, to_apply=%region_21.22 | all-reduce | flops 9216 | bytes 73728 | tf_op jit(solution)/shard_map/psum | solution.py:302
  691.7 32.7 %reduce-scatter.29.cloned.1.call-done = f32[1536,48]{0,1:T(8,128)} async-done(((f32[1536,768]{0,1:T(8,128)}), f32[1536,48]{0,1:T(8,128)}) %reduce-scatter.29.cloned.1.call-update) | async-done | bytes 294928 | tf_op jit(solution)/shard_map/reduce_scatter | solution.py:295
  724.4 79.0 %reduce-scatter.27.cloned.1.call-done = f32[48,1536]{1,0:T(8,128)} async-done(((f32[768,1536]{1,0:T(8,128)}), f32[48,1536]{1,0:T(8,128)}) %reduce-scatter.27.cloned.1.call-update) | async-done | bytes 294928 | tf_op jit(solution)/shard_map/reduce_scatter | solution.py:294
  803.4 61.9 %reduce-scatter.25.cloned.1.call-done = f32[384,48]{0,1:T(8,128)} async-done(((f32[384,768]{0,1:T(8,128)}), f32[384,48]{0,1:T(8,128)}) %reduce-scatter.25.cloned.1.call-update) | async-done | bytes 73744 | tf_op jit(solution)/shard_map/reduce_scatter | solution.py:293
  865.3 61.4 %reduce-scatter.35.cloned.1.call-done = f32[48,384]{1,0:T(8,128)} async-done(((f32[768,384]{1,0:T(8,128)}), f32[48,384]{1,0:T(8,128)}) %reduce-scatter.35.cloned.1.call-update) | async-done | bytes 73744
  926.7 61.6 %reduce-scatter.31.cloned.1.call-done = f32[48,384]{1,0:T(8,128)} async-done(((f32[768,384]{1,0:T(8,128)}), f32[48,384]{1,0:T(8,128)}) %reduce-scatter.31.cloned.1.call-update) | async-done | bytes 73744
  988.3 61.4 %reduce-scatter.33.cloned.1.call-done = f32[48,384]{1,0:T(8,128)} async-done(((f32[768,384]{1,0:T(8,128)}), f32[48,384]{1,0:T(8,128)}) %reduce-scatter.33.cloned.1.call-update) | async-done | bytes 73744
  (291 shorter events, 203.3 us)
Async XLA Ops:
  8.0 87.8 %all-gather.8.cloned.1.call-start = ((), (), s32[]{:S(2)}) async-start(), calls=%async_computation.10 | async-start | bytes 2359296 | tf_op jit(solution)/shard_map/all_gather | solution.py:152
  8.8 172.7 %reduce-scatter.17.cloned.1.call-start = ((), (), s32[]{:S(2)}) async-start(), calls=%async_computation.11 | async-start | bytes 4718592 | tf_op jit(solution)/shard_map/reduce_scatter | solution.py:173
  139.4 46.1 %all-gather.12.cloned.1.call-start = ((), (), s32[]{:S(2)}) async-start(), calls=%async_computation.13 | async-start | bytes 2506752 | tf_op jit(solution)/shard_map/all_gather | solution.py:149
  140.0 71.9 %all-gather.10.cloned.1.call-start = ((), (), s32[]{:S(2)}) async-start(), calls=%async_computation.12 | async-start | bytes 2359296 | tf_op jit(solution)/shard_map/all_gather | solution.py:176
  184.7 72.0 %all-gather.14.cloned.1.call-start = ((), (), s32[]{:S(2)}) async-start(), calls=%async_computation.14 | async-start | bytes 2506752 | tf_op jit(solution)/shard_map/all_gather | solution.py:150
  185.3 120.3 %reduce-scatter.19.cloned.1.call-start = ((), (), s32[]{:S(2)}) async-start(), calls=%async_computation.15 | async-start | bytes 4718592 | tf_op jit(solution)/shard_map/reduce_scatter | solution.py:180
  263.6 131.2 %all-gather.16.cloned.1.call-start = ((), (), s32[]{:S(2)}) async-start(), calls=%async_computation.16 | async-start | bytes 2359296 | tf_op jit(solution)/shard_map/all_gather | solution.py:222
  313.5 94.9 %all-gather.18.cloned.1.call-start = ((), (), s32[]{:S(2)}) async-start(), calls=%async_computation.17 | async-start | bytes 2506752 | tf_op jit(solution)/shard_map/all_gather | solution.py:219
  313.6 7.3 collective-permute-start
  320.9 7.3 collective-permute-start.1
  320.9 7.3 collective-permute-start.8
  328.2 7.4 collective-permute-start.2
  328.2 7.4 collective-permute-start.9
  335.6 7.4 collective-permute-start.3
  335.6 7.4 collective-permute-start.10
  342.9 7.4 collective-permute-start.4
  342.9 7.4 collective-permute-start.11
  350.3 7.5 collective-permute-start.5
  350.3 7.5 collective-permute-start.12
  357.8 7.7 collective-permute-start.6
  357.8 7.7 collective-permute-start.13
  365.5 7.6 collective-permute-start.7
  365.5 91.8 %reduce-scatter.21.cloned.1.call-start = ((), (), s32[]{:S(2)}) async-start(), calls=%async_computation.18 | async-start | bytes 4718592 | tf_op jit(solution)/shard_map/reduce_scatter | solution.py:238
  365.6 24.8 %collective-permute-start.14 = (bf16[1536,48]{0,1:T(8,128)(2,1)}, bf16[1536,48]{0,1:T(8,128)(2,1)S(1)}, u32[]{:S(2)}, u32[]{:S(2)}) collective-permute-start(bf16[1536,48]{0,1:T(8,128)(2,1)} %collective-permute-done.13), channel_id=1, source_target_pairs={{2,0},{4,2},{6,4},{8,6},{10,8},{12,10},{14,12},{16,14},{18,16},{20... | collective-permute-start | bytes 442376 | tf_op jit(solution)/shard_map/ppermute | solution.py:203
  415.3 134.8 %all-gather.20.cloned.1.call-start = ((), (), s32[]{:S(2)}) async-start(), calls=%async_computation.19 | async-start | bytes 2359296 | tf_op jit(solution)/shard_map/all_gather | solution.py:244
  464.1 225.1 %reduce-scatter.23.cloned.1.call-start = ((), (), s32[]{:S(2)}) async-start(), calls=%async_computation.20 | async-start | bytes 2359296 | tf_op jit(solution)/shard_map/reduce_scatter | solution.py:286
  620.2 104.2 %reduce-scatter.29.cloned.1.call-start = ((), (), s32[]{:S(2)}) async-start(), calls=%async_computation.23 | async-start | bytes 5013504 | tf_op jit(solution)/shard_map/reduce_scatter | solution.py:295
  627.4 176.0 %reduce-scatter.27.cloned.1.call-start = ((), (), s32[]{:S(2)}) async-start(), calls=%async_computation.22 | async-start | bytes 5013504 | tf_op jit(solution)/shard_map/reduce_scatter | solution.py:294
  634.7 230.6 %reduce-scatter.25.cloned.1.call-start = ((), (), s32[]{:S(2)}) async-start(), calls=%async_computation.21 | async-start | bytes 1253376 | tf_op jit(solution)/shard_map/reduce_scatter | solution.py:293
  639.3 287.4 %reduce-scatter.35.cloned.1.call-start = ((), (), s32[]{:S(2)}) async-start(), calls=%async_computation.26 | async-start | bytes 1253376
  643.0 345.3 %reduce-scatter.31.cloned.1.call-start = ((), (), s32[]{:S(2)}) async-start(), calls=%async_computation.24 | async-start | bytes 1253376
  645.4 404.3 %reduce-scatter.33.cloned.1.call-start = ((), (), s32[]{:S(2)}) async-start(), calls=%async_computation.25 | async-start | bytes 1253376
  (52 other events, 713.3 us)
Sparse Core Ops, SparseCore 0:
  10.4 29.8 all-gather.7
  139.5 41.8 reduce-scatter.16
  263.7 41.7 reduce-scatter.18
  415.5 41.7 reduce-scatter.20
Sparse Core Ops, SparseCore 1:
  142.1 40.8 all-gather.11
  185.0 26.8 all-gather.9
  214.0 42.6 all-gather.13
  313.6 27.0 all-gather.15
  365.6 42.8 all-gather.17
  464.1 27.0 all-gather.19
  620.3 23.6 reduce-scatter.22
  648.2 76.1 reduce-scatter.28
  728.7 74.7 reduce-scatter.26
  807.6 57.6 reduce-scatter.24
  869.4 57.3 reduce-scatter.34
  930.9 57.3 reduce-scatter.30
  992.4 57.3 reduce-scatter.32
